TPU v7x, 32 devices: a whole 2x2x4 slice. The times are simulated.
32 devices in a mesh: ctx: 4 (over x, core), dp: 2 (over y), tp: 4 (over z).
Axes of the slice: x: 2, y: 2, z: 4, core: 2. Of those that a mesh axis runs over, the one named last changes fastest.
Arguments:
- token_ids: int32 [4, 4], replicated, may hold values from 0 to 50279
- decode_prompt: int32 [4], replicated, may hold values from 0 to 3, as said below
- embedding: bfloat16 [50280, 4096], P('dp', ('ctx', 'tp')), may hold values from -6 to 6
- norm_gain: float32 [4096], replicated, may hold values from 0.1 to 1.9
- w_zx: bfloat16 [2, 128, 64, 4096], P(None, ('tp', 'ctx')), may hold values from -0.09375 to 0.09375
- w_bcdt: bfloat16 [4096, 384], P(None, ('ctx', 'tp')), may hold values from -0.09375 to 0.09375
- conv_x_weight: float32 [4, 128, 64], P(None, ('tp', 'ctx')), may hold values from -3 to 3
- conv_x_bias: float32 [128, 64], P(('tp', 'ctx')), may hold values from -3 to 3
- conv_bc_weight: float32 [4, 256], replicated, may hold values from -3 to 3
- conv_bc_bias: float32 [256], replicated, may hold values from -3 to 3
- dt_bias: float32 [128], P(('tp', 'ctx')), may hold values from -4 to -1
- a_log: float32 [128], P(('tp', 'ctx')), may hold values from 0 to 2.7
- d_skip: float32 [128], P(('tp', 'ctx')), may hold values from 0.5 to 1.5
- gate_norm_gain: float32 [128, 64], P(('tp', 'ctx')), may hold values from 0.1 to 1.9
- w_out: bfloat16 [128, 64, 4096], P(('tp', 'ctx')), may hold values from -0.0625 to 0.0625
- state_parts: bfloat16 [4, 4, 128, 64, 128], P('ctx', 'dp', 'tp'), may hold values from -6 to 6
- seg_rate: float32 [4, 4, 128], P('ctx', 'dp', 'tp'), may hold values from 0 to 4
- x_tail: bfloat16 [4, 3, 128, 64], P('dp', None, ('tp', 'ctx')), may hold values from -6 to 6
- bc_tail: bfloat16 [4, 3, 256], P('dp'), may hold values from -6 to 6
Outputs:
- mixer_out: bfloat16 [4, 4, 4096], P(None, 'dp', ('ctx', 'tp'))
- final_state: float32 [4, 128, 64, 128], P('dp', ('tp', 'ctx'))
Inputs may be any that keep to these rules, and one draw needn't show every extreme that they name: decode_prompt is a permutation of the prompts; slot s is decoded by dp group s // 2, and prompt q is held by dp group q // 2; the 2 prompts held by one dp group are decoded by 2 different dp groups.
All inputs are finite; a program needn't handle non-finite values.
Results may differ from a plain program's by a relative error of at most 0.02.
Values may be sent and summed in bfloat16 or wider, within the bound.
A program may use at most 64 MiB of HBM per device.

v0:
```python
import jax
import jax.numpy as jnp
from jax import lax
from jax.sharding import PartitionSpec as P

HEADS = 128
HEAD_DIM = 64
epsilon = 1e-05


def entering(shard, axis, combine, identity):
    count, here = (lax.axis_size(axis), lax.axis_index(axis))
    everything = lax.all_gather(shard, axis)
    start = jnp.broadcast_to(jnp.asarray(identity, shard.dtype), shard.shape)

    def step(k, before):
        at = count - 1 - k
        reached = at > here
        new = combine(before, everything[at])
        return jnp.where(reached, new, before)

    return lax.fori_loop(0, count, step, start)


def rms_scale(values, gain):
    return values * lax.rsqrt(jnp.mean(values * values, axis=-1, keepdims=True) + epsilon) * gain


def select_rows(picker, values):
    return jnp.tensordot(picker, values, axes=1, precision=lax.Precision.HIGHEST)


def add_rates(earlier, later_one):
    return earlier + later_one


def per_device(
    token_ids,
    decode_prompt,
    embedding,
    norm_gain,
    w_zx,
    w_bcdt,
    conv_x_weight,
    conv_x_bias,
    conv_bc_weight,
    conv_bc_bias,
    dt_bias,
    a_log,
    d_skip,
    gate_norm_gain,
    w_out,
    state_parts,
    seg_rate,
    x_tail,
    bc_tail,
):
    group = lax.axis_index("dp")
    local_count = state_parts.shape[1]
    slot_count = decode_prompt.shape[0]
    head_count = w_zx.shape[1]
    state_width = conv_bc_bias.shape[0] // 2
    after_rates = entering(seg_rate, "ctx", add_rates, jnp.zeros_like(seg_rate))
    seg_weight = jnp.exp(-after_rates[0])
    scaled = seg_weight[:, :, None, None] * state_parts[0].astype(jnp.float32)
    channel_sums = lax.psum_scatter(
        scaled.astype(jnp.bfloat16), "ctx", scatter_dimension=2, tiled=True
    ).astype(jnp.float32)
    combined = lax.all_to_all(
        channel_sums.astype(jnp.bfloat16), "ctx", split_axis=1, concat_axis=2, tiled=True
    ).astype(channel_sums.dtype)
    tails_x = x_tail.astype(jnp.float32)
    tails_bc = bc_tail.astype(jnp.float32)
    own_slots = lax.dynamic_slice_in_dim(decode_prompt, group * local_count, local_count)
    prompt_ids = jnp.arange(slot_count, dtype=jnp.int32)
    every_state, every_x, every_bc = (
        lax.all_gather(combined.astype(jnp.bfloat16), "dp", axis=0, tiled=True).astype(
            combined.dtype
        ),
        lax.all_gather(tails_x.astype(jnp.bfloat16), "dp", axis=0, tiled=True).astype(
            tails_x.dtype
        ),
        lax.all_gather(tails_bc.astype(jnp.bfloat16), "dp", axis=0, tiled=True).astype(
            tails_bc.dtype
        ),
    )
    picker = (own_slots[:, None] == prompt_ids[None, :]).astype(jnp.float32)
    ssm_state = select_rows(picker, every_state)
    x_window = select_rows(picker, every_x)
    bc_window = select_rows(picker, every_bc)
    vocab_rows = embedding.shape[0]
    holder = (decode_prompt[:, None] == prompt_ids[None, :]).astype(jnp.int32)
    slot_tokens = jnp.sum(token_ids[:, None, :] * holder[None], axis=2)
    offset_tokens = slot_tokens - group * vocab_rows
    inside = (offset_tokens >= 0) & (offset_tokens < vocab_rows)
    looked = jnp.take(embedding, jnp.clip(offset_tokens, 0, vocab_rows - 1), axis=0)
    partial_rows = jnp.where(inside[..., None], looked.astype(jnp.float32), 0.0)
    own_rows = lax.psum_scatter(
        partial_rows.astype(jnp.bfloat16), "dp", scatter_dimension=1, tiled=True
    )
    embedded = lax.all_gather(own_rows, ("ctx", "tp"), axis=2, tiled=True)
    steps_count = embedded.shape[0]
    flat_rows = embedded.reshape(-1, embedded.shape[2]).astype(jnp.float32)
    normed = rms_scale(flat_rows, norm_gain).astype(jnp.bfloat16)
    projected = jnp.einsum("rd,khed->krhe", normed, w_zx, preferred_element_type=jnp.float32)
    projected = projected.reshape(
        2, steps_count, local_count, projected.shape[2], projected.shape[3]
    )
    columns = lax.all_gather(
        jnp.dot(normed, w_bcdt, preferred_element_type=jnp.float32),
        ("ctx", "tp"),
        axis=1,
        tiled=True,
    )
    columns = columns.reshape(steps_count, local_count, -1)
    head_block = lax.axis_index("tp") * lax.axis_size("ctx") + lax.axis_index("ctx")
    head_start = 2 * state_width + head_block * head_count
    dt_raw = lax.dynamic_slice_in_dim(columns, head_start, head_count, 2)
    decay_rate = -jnp.exp(a_log)
    gated_steps = []
    for moment in range(steps_count):
        x_window = jnp.concatenate([x_window, projected[1, moment][:, None]], axis=1)
        bc_window = jnp.concatenate(
            [bc_window, columns[moment, :, None, : 2 * state_width]], axis=1
        )
        x_conv = jax.nn.silu(jnp.einsum("pkhe,khe->phe", x_window, conv_x_weight) + conv_x_bias)
        bc_conv = jax.nn.silu(jnp.einsum("pkn,kn->pn", bc_window, conv_bc_weight) + conv_bc_bias)
        step_size = jax.nn.softplus(dt_raw[moment] + dt_bias)
        retain = jnp.exp(step_size * decay_rate)
        ssm_state = (
            retain[:, :, None, None] * ssm_state
            + (step_size[:, :, None] * x_conv)[:, :, :, None] * bc_conv[:, None, None, :state_width]
        )
        output = (
            jnp.einsum("phen,pn->phe", ssm_state, bc_conv[:, state_width:])
            + d_skip[None, :, None] * x_conv
        )
        gated_steps.append(output * jax.nn.silu(projected[0, moment]))
        x_window = x_window[:, 1:]
        bc_window = bc_window[:, 1:]
    gated_all = jnp.stack(gated_steps)
    local_squares = jnp.sum(gated_all * gated_all, axis=(2, 3))
    total_squares = lax.psum(local_squares, ("ctx", "tp"))
    inverse = lax.rsqrt(total_squares / (HEADS * HEAD_DIM) + epsilon)
    normed_out = (gated_all * inverse[:, :, None, None] * gate_norm_gain).astype(jnp.bfloat16)
    partial_out = jnp.einsum("tphe,hed->tpd", normed_out, w_out, preferred_element_type=jnp.float32)
    outer_sum = lax.psum_scatter(
        partial_out.astype(jnp.bfloat16), "ctx", scatter_dimension=2, tiled=True
    ).astype(jnp.float32)
    mixed = lax.psum_scatter(outer_sum, "tp", scatter_dimension=2, tiled=True)
    return (mixed.astype(jnp.bfloat16), ssm_state)


def solution(mesh):
    return jax.shard_map(
        per_device,
        mesh=mesh,
        in_specs=(
            P(),
            P(),
            P("dp", ("ctx", "tp")),
            P(),
            P(None, ("tp", "ctx"), None, None),
            P(None, ("ctx", "tp")),
            P(None, ("tp", "ctx"), None),
            P(("tp", "ctx"), None),
            P(),
            P(),
            P(("tp", "ctx")),
            P(("tp", "ctx")),
            P(("tp", "ctx")),
            P(("tp", "ctx"), None),
            P(("tp", "ctx"), None, None),
            P("ctx", "dp", "tp", None, None),
            P("ctx", "dp", "tp"),
            P("dp", None, ("tp", "ctx"), None),
            P("dp", None, None),
        ),
        out_specs=(P(None, "dp", ("ctx", "tp")), P("dp", ("tp", "ctx"), None, None)),
        check_vma=False,
    )
```

profile of v0, /device:TPU:0, one launch (start us, length us, event | category | flops | bytes accessed | tf_op | source)
XLA Modules:
  0.0 232.6 jit_solution(4422377353734788636)
XLA Ops:
  7.3 6.4 %all-gather = f32[4,2,32]{2,1,0:T(2,128)S(1)} all-gather(f32[1,2,32]{2,1,0:T(2,128)} %param.37), channel_id=2, replica_groups=mesh['ctx'=4,'dp'=2,'tp'=4] {'ctx'}, dimensions={0}, use_global_device_ids=true | all-gather | bytes 1280 | tf_op jit(solution)/shard_map/all_gather | solution.py:13
  13.7 0.1 while.16
  13.8 0.1 copy.185
  13.9 2.5 %fusion.2 = bf16[2,32,64,128]{3,2,0,1:T(8,128)(2,1)} fusion(bf16[1,2,32,64,128]{4,3,2,1,0:T(8,128)(2,1)} %param.36, f32[2,32]{0,1:T(8,128)S(1)} %copy.185), kind=kLoop, calls=%fused_computation.6 | loop fusion | flops 1572864 | bytes 2097408 | tf_op jit(solution)/shard_map/convert_element_type | solution.py:67
  16.4 0.7 fusion.65
  17.1 0.8 multiply_reduce_fusion.2
  18.0 0.1 reshape.339
  18.1 0.1 copy.177
  18.2 0.1 copy.178
  18.3 6.9 %gather_fusion = bf16[16,256]{1,0:T(8,128)(2,1)S(1)} fusion(bf16[25140,256]{1,0:T(8,128)(2,1)} %param.23, s32[1024]{0:T(1024)S(1)} %pad_clamp_fusion), kind=kCustom, calls=%fused_computation | custom fusion | bytes 16448 | tf_op jit(solution)/shard_map/jit(_take)/gather | solution.py:96
  25.2 0.1 select_convert_fusion
  25.3 5.0 %all-reduce = bf16[4,4,256]{2,0,1:T(4,128)(2,1)S(1)} all-reduce(bf16[4,4,256]{2,0,1:T(4,128)(2,1)S(1)} %select_convert_fusion), channel_id=3, replica_groups=mesh['ctx'=4,'dp'=2,'tp'=4] {'dp'}, use_global_device_ids=true, to_apply=%region_1.2.clone | all-reduce | flops 4096 | bytes 16384
  30.3 1.2 dynamic-slice
  32.2 32.8 %all_gather.21 = bf16[4,2,4096]{2,0,1:T(4,128)(2,1)S(1)} all-gather(bf16[4,2,256]{2,0,1:T(4,128)(2,1)S(1)} %constant_dynamic-slice_fusion), channel_id=1, replica_groups=mesh['ctx'=4,'dp'=2,'tp'=4] {'ctx','tp'}, dimensions={2}, use_global_device_ids=true | all-gather | bytes 69632 | tf_op jit(solution)/shard_map/all_gather | solution.py:101
  65.0 0.1 multiply_reduce_fusion
  65.2 0.7 dynamic_slice.17
  66.0 0.7 exponential_negate_fusion
  66.6 4.6 %all_gather.26 = bf16[4,3,8,64]{3,2,1,0:T(8,128)(2,1)S(1)} all-gather(bf16[2,3,8,64]{3,2,1,0:T(8,128)(2,1)} %param.38), channel_id=1, replica_groups=mesh['ctx'=4,'dp'=2,'tp'=4] {'dp'}, dimensions={0}, use_global_device_ids=true | all-gather | bytes 18432 | tf_op jit(solution)/shard_map/all_gather | solution.py:80
  71.2 0.1 copy.181
  71.3 0.1 rsqrt.15
  71.4 0.1 reshape.335
  71.5 0.2 convolution_bitcast_fusion.2
  71.8 6.8 %convolution_bitcast_fusion.1 = f32[2,8,8,64]{3,1,2,0:T(8,128)S(1)} fusion(bf16[2,8,64,4096]{3,2,1,0:T(8,128)(2,1)} %param.25, f32[8,4096]{1,0:T(8,128)S(1)} %reshape.335, f32[4096]{0:T(1024)S(1)} %copy-done.2, f32[8]{0:T(128)S(1)} %rsqrt.15), kind=kOutput, calls=%fused_computation.9 | convolution fusion | flops 67207168 | bytes 8568864 | tf_op jit(solution)/shard_map/rd,khed->krhe/dot_general | solution.py:105
  78.6 28.9 %all-gather.1 = f32[16,24,8]{1,2,0:T(8,128)S(1)} all-gather(f32[1,24,8]{1,2,0:T(8,128)S(1)} %convolution_bitcast_fusion.2), channel_id=1, replica_groups=mesh['ctx'=4,'dp'=2,'tp'=4] {'ctx','tp'}, dimensions={0}, use_global_device_ids=true | all-gather | bytes 13056 | tf_op jit(solution)/shard_map/all_gather | solution.py:109
  107.6 0.1 reshape.348
  107.7 0.2 fusion.26
  107.9 0.1 multiply_exponential_fusion.3
  108.1 0.1 copy.183
  108.2 0.1 copy.195
  108.3 0.1 copy.198
  108.3 0.1 copy.201
  108.5 0.1 fusion.19
  108.6 0.1 broadcast_multiply_fusion.3
  108.7 0.2 copy.192
  108.8 0.2 copy.197
  109.0 0.2 copy.200
  109.2 0.2 copy.203
  109.3 4.4 %all_gather.27 = bf16[4,3,256]{2,1,0:T(4,128)(2,1)S(1)} all-gather(bf16[2,3,256]{2,1,0:T(4,128)(2,1)S(1)} %copy.193), channel_id=1, replica_groups=mesh['ctx'=4,'dp'=2,'tp'=4] {'dp'}, dimensions={0}, use_global_device_ids=true | all-gather | bytes 9216 | tf_op jit(solution)/shard_map/all_gather | solution.py:83
  113.7 0.2 fusion.55
  114.0 3.4 %all-to-all-start = ((bf16[2,32,16,128]{3,2,0,1:T(8,128)(2,1)}), bf16[2,32,16,128]{3,2,0,1:T(8,128)(2,1)S(1)}, u32[]{:S(2)}, u32[]{:S(2)}) async-start(bf16[2,32,16,128]{3,2,0,1:T(8,128)(2,1)} %reduce-scatter.8.cloned.1.call-done), calls=%async_computation.1 | async-start | bytes 524288 | tf_op jit(solution)/shard_map/all_to_all | solution.py:69
  117.5 5.9 %all-to-all-done = bf16[2,32,16,128]{3,2,0,1:T(8,128)(2,1)S(1)} async-done(((bf16[2,32,16,128]{3,2,0,1:T(8,128)(2,1)}), bf16[2,32,16,128]{3,2,0,1:T(8,128)(2,1)S(1)}, u32[]{:S(2)}, u32[]{:S(2)}) %all-to-all-start) | async-done | bytes 262176 | tf_op jit(solution)/shard_map/all_to_all | solution.py:69
  123.4 8.4 %all_gather.25 = bf16[4,8,64,128]{3,2,1,0:T(8,128)(2,1)S(1)} all-gather(bf16[2,8,64,128]{3,2,1,0:T(8,128)(2,1)S(1)} %bitcast.312), channel_id=1, replica_groups=mesh['ctx'=4,'dp'=2,'tp'=4] {'dp'}, dimensions={0}, use_global_device_ids=true | all-gather | bytes 786432 | tf_op jit(solution)/shard_map/all_gather | solution.py:77
  131.9 3.2 %multiply_add_fusion = (f32[2,8,64,128]{3,0,2,1:T(2,128)S(1)}, bf16[2,8,64,128]{3,0,2,1:T(2,128)(2,1)S(1)}, bf16[2,8,64,128]{3,0,2,1:T(2,128)(2,1)S(1)}, bf16[2,8,64,128]{3,0,2,1:T(2,128)(2,1)S(1)}) fusion(f32[2,128]{1,0:T(2,128)S(1)} %get-tuple-element.228, f32[2,8,64]{0,2,1:T(8,128)S(1)} %copy.203, f32[2,8]{0,1:T(8,128)S(1)} %copy.201, ...), kind=kOutput, calls=%fused_computation.17 | convolution fusion | flops 3014664 | bytes 1855752 | tf_op jit(solution)/shard_map/dot_general | solution.py:30
  135.1 0.3 fusion.81
  135.4 0.3 fusion.4
  135.7 0.3 fusion.6
  136.1 0.3 fusion.8
  136.4 0.1 multiply_bitcast_fusion.3
  136.5 0.1 multiply_reduce_fusion.1
  136.6 0.1 copy.204
  136.7 31.9 %psum.7 = f32[4,2]{0,1:T(2,128)S(1)} all-reduce(f32[4,2]{0,1:T(2,128)S(1)} %copy.204), channel_id=1, replica_groups=mesh['ctx'=4,'dp'=2,'tp'=4] {'ctx','tp'}, use_global_device_ids=true, to_apply=%region_7.8 | all-reduce | flops 8 | bytes 64 | tf_op jit(solution)/shard_map/psum | solution.py:143
  168.6 0.1 copy.205
  168.7 2.9 %fusion = bf16[4,2,4096]{2,0,1:T(4,128)(2,1)S(1)} fusion(bf16[8,64,4096]{2,1,0:T(8,128)(2,1)} %param.35, bf16[4,2,8,64]{3,2,1,0:T(8,128)(2,1)S(1)} %multiply_convert_fusion.1), kind=kOutput, calls=%fused_computation.3 | convolution fusion | flops 33587200 | bytes 4268032 | tf_op jit(solution)/shard_map/tphe,hed->tpd/dot_general | solution.py:146
  171.7 2.9 %copy.279 = bf16[4,2,4096]{0,1,2:T(2,128)(2,1)S(1)} copy(bf16[4,2,4096]{2,0,1:T(4,128)(2,1)S(1)} %fusion) | data formatting | bytes 131072
  174.6 1.8 reshape.378
  176.5 22.4 %reduce-scatter.10.cloned.1.call-done = bf16[1024,8]{1,0:T(8,128)(2,1)} async-done(((bf16[4096,8]{1,0:T(8,128)(2,1)}), bf16[1024,8]{1,0:T(8,128)(2,1)}) %reduce-scatter.10.cloned.1.call-update) | async-done | bytes 16400
  198.9 1.2 reshape.379
  200.1 0.4 copy.280
  200.5 0.5 copy.281
  200.9 1.4 reshape.380
  202.4 22.0 %reduce-scatter.12.cloned.1.call-done = f32[256,8]{1,0:T(8,128)} async-done(((f32[1024,8]{1,0:T(8,128)}), f32[256,8]{1,0:T(8,128)}) %reduce-scatter.12.cloned.1.call-update) | async-done | bytes 8208
  224.4 1.0 reshape.381
  225.4 0.1 copy.282
  225.5 0.6 copy.207
  (64 shorter events, 0.8 us)
Async XLA Ops:
  7.2 64.3 %copy-start = (bf16[4096,24]{0,1:T(8,128)(2,1)S(1)}, bf16[4096,24]{0,1:T(8,128)(2,1)}, u32[]{:S(2)}) copy-start(bf16[4096,24]{0,1:T(8,128)(2,1)} %param.26) | copy-start | bytes 589828
  7.2 64.3 %copy-start.2 = (f32[4096]{0:T(1024)S(1)}, f32[4096]{0:T(1024)}, u32[]{:S(2)}) copy-start(f32[4096]{0:T(1024)} %param.24) | copy-start | bytes 49156
  7.2 106.8 %reduce-scatter.8.cloned.1.call-start = ((), (), s32[]{:S(2)}) async-start(), calls=%async_computation.4 | async-start | bytes 1310720 | tf_op jit(solution)/shard_map/reduce_scatter | solution.py:66
  71.8 36.2 %copy-start.10 = (f32[8]{0:T(128)S(1)}, f32[8]{0:T(128)}, u32[]{:S(2)}) copy-start(f32[8]{0:T(128)} %param.31) | copy-start | bytes 100
  71.8 36.3 %copy-start.7 = (bf16[2,3,256]{2,0,1:T(2,128)(2,1)S(1)}, bf16[2,3,256]{2,0,1:T(2,128)(2,1)}, u32[]{:S(2)}) copy-start(bf16[2,3,256]{2,0,1:T(2,128)(2,1)} %param.39) | copy-start | bytes 9220
  71.8 36.7 %copy-start.4 = (f32[4,8,64]{2,1,0:T(8,128)S(1)}, f32[4,8,64]{2,1,0:T(8,128)}, u32[]{:S(2)}) copy-start(f32[4,8,64]{2,1,0:T(8,128)} %param.27) | copy-start | bytes 24580
  71.8 36.8 %copy-start.3 = (f32[8,64]{1,0:T(8,128)S(1)}, f32[8,64]{1,0:T(8,128)}, u32[]{:S(2)}) copy-start(f32[8,64]{1,0:T(8,128)} %param.28) | copy-start | bytes 6148
  71.8 42.1 %copy-start.6 = (f32[4,256]{1,0:T(4,128)S(1)}, f32[4,256]{1,0:T(4,128)}, u32[]{:S(2)}) copy-start(f32[4,256]{1,0:T(4,128)} %param.29) | copy-start | bytes 12292
  71.8 42.2 %copy-start.8 = (f32[256]{0:T(256)S(1)}, f32[256]{0:T(256)}, u32[]{:S(2)}) copy-start(f32[256]{0:T(256)} %param.30) | copy-start | bytes 3076
  114.0 9.4 %all-to-all-start = ((bf16[2,32,16,128]{3,2,0,1:T(8,128)(2,1)}), bf16[2,32,16,128]{3,2,0,1:T(8,128)(2,1)S(1)}, u32[]{:S(2)}, u32[]{:S(2)}) async-start(bf16[2,32,16,128]{3,2,0,1:T(8,128)(2,1)} %reduce-scatter.8.cloned.1.call-done), calls=%async_computation.1 | async-start | bytes 524288 | tf_op jit(solution)/shard_map/all_to_all | solution.py:69
  117.5 81.4 %reduce-scatter.10.cloned.1.call-start = ((), (), s32[]{:S(2)}) async-start(), calls=%async_computation.5 | async-start | bytes 1310720
  131.9 4.5 %copy-start.9 = (f32[8]{0:T(128)S(1)}, f32[8]{0:T(128)}, u32[]{:S(2)}) copy-start(f32[8]{0:T(128)} %param.33) | copy-start | bytes 100
  131.9 36.8 %copy-start.5 = (f32[8,64]{1,0:T(8,128)S(1)}, f32[8,64]{1,0:T(8,128)}, u32[]{:S(2)}) copy-start(f32[8,64]{1,0:T(8,128)} %param.34) | copy-start | bytes 6148
  135.1 39.5 %copy-start.1 = (f32[2,8,64,128]{3,2,1,0:T(8,128)}, f32[2,8,64,128]{3,2,1,0:T(8,128)S(1)}, u32[]{:S(2)}) copy-start(f32[2,8,64,128]{3,2,1,0:T(8,128)S(1)} %copy.208) | copy-start | bytes 1572868
  176.4 48.0 %reduce-scatter.12.cloned.1.call-start = ((), (), s32[]{:S(2)}) async-start(), calls=%async_computation.6 | async-start | bytes 655360
Sparse Core Ops, SparseCore 0:
  16.5 26.5 reduce-scatter.7
  176.5 22.3 reduce-scatter.9
  202.5 21.8 reduce-scatter.11
where the time goes:
time: 233 us
  blocking collectives  122 us (52%)
  waiting for transfers between devices  50.4 us (22%)
  local copies, waits for them, and re-layouts  20.9 us (9%)
  between operations  14.8 us (6%)
  matrix products  14.7 us (6%)
  other arithmetic  5.73 us (2%)
  starting transfers between devices  3.54 us (2%)
    unnamed x5, waiting for transfers between devices  44.5 us
    all_gather x1, blocking collectives, per_device(): embedded = lax.all_gather(own_rows, ('ctx', 'tp'), axis=2, tiled=True)  32.8 us
    psum x1, blocking collectives, per_device(): total_squares = lax.psum(local_squares, ('ctx', 'tp'))  31.9 us
    all_gather x1, blocking collectives, per_device(): lax.all_gather(jnp.dot(normed, w_bcdt, preferred_element_type=jnp.float32...  28.9 us
    unnamed x36, local copies, waits for them, and re-layouts  11.3 us
    all_gather x1, blocking collectives, per_device(): lax.all_gather(combined.astype(jnp.bfloat16), 'dp', axis=0, tiled=True)  8.41 us
    gather x2, local copies, waits for them, and re-layouts, per_device(): jnp.take(embedding, jnp.clip(offset_tokens, 0, vocab_rows - 1), axis=0)  6.9 us
    dot_general x1, matrix products, per_device(): jnp.einsum('rd,khed->krhe', normed, w_zx, preferred_element_type=jnp.floa...  6.79 us
  transfers between devices with their start and end apart: 4, of which 3 were waited for; matrix products, arithmetic and copies ran while one was open for 9% of the time, Pallas kernels for 0%

commit v1 on v0

--- a/solution.py
+++ b/solution.py
@@ -140,7 +140,9 @@
         bc_window = bc_window[:, 1:]
     gated_all = jnp.stack(gated_steps)
     local_squares = jnp.sum(gated_all * gated_all, axis=(2, 3))
-    total_squares = lax.psum(local_squares, ("ctx", "tp"))
+    total_squares = local_squares
+    for mesh_axis in ("tp", "ctx"):
+        total_squares = lax.psum(total_squares, mesh_axis)
     inverse = lax.rsqrt(total_squares / (HEADS * HEAD_DIM) + epsilon)
     normed_out = (gated_all * inverse[:, :, None, None] * gate_norm_gain).astype(jnp.bfloat16)
     partial_out = jnp.einsum("tphe,hed->tpd", normed_out, w_out, preferred_element_type=jnp.float32)

time: 233 us -> 218 us (0.936)
  blocking collectives: 122 us -> 107 us
    psum x1 -> x2, blocking collectives: 31.9 us -> 16.3 us  [per_device(): total_squares = lax.psum(total_squares, mesh_axis)]
  transfers between devices with their start and end apart: 4 -> 4, of which waited for: 3 -> 3; matrix products, arithmetic and copies ran while one was open for 9% -> 10% of each run, Pallas kernels for 0% -> 0%
where the time goes in v1:
time: 218 us; the launch traced here: 217 us
  blocking collectives  107 us (49%)
  waiting for transfers between devices  50.3 us (23%)
  local copies, waits for them, and re-layouts  20.9 us (10%)
  between operations  14.9 us (7%)
  matrix products  14.7 us (7%)
  other arithmetic  5.73 us (3%)
  starting transfers between devices  3.54 us (2%)
    unnamed x5, waiting for transfers between devices  44.4 us
    all_gather x1, blocking collectives, per_device(): embedded = lax.all_gather(own_rows, ('ctx', 'tp'), axis=2, tiled=True)  32.8 us
    all_gather x1, blocking collectives, per_device(): lax.all_gather(jnp.dot(normed, w_bcdt, preferred_element_type=jnp.float32...  28.9 us
    psum x2, blocking collectives, per_device(): total_squares = lax.psum(total_squares, mesh_axis)  16.3 us
    unnamed x36, local copies, waits for them, and re-layouts  11.3 us
    all_gather x1, blocking collectives, per_device(): lax.all_gather(combined.astype(jnp.bfloat16), 'dp', axis=0, tiled=True)  8.41 us
    gather x2, local copies, waits for them, and re-layouts, per_device(): jnp.take(embedding, jnp.clip(offset_tokens, 0, vocab_rows - 1), axis=0)  6.9 us
    dot_general x1, matrix products, per_device(): jnp.einsum('rd,khed->krhe', normed, w_zx, preferred_element_type=jnp.floa...  6.79 us
  transfers between devices with their start and end apart: 4, of which 3 were waited for; matrix products, arithmetic and copies ran while one was open for 10% of the time, Pallas kernels for 0%

profile of v1, /device:TPU:0, one launch (start us, length us, event | category | flops | bytes accessed | tf_op | source)
XLA Modules:
  0.0 216.9 jit_solution(2263262972092331855)
XLA Ops:
  7.3 6.4 %all-gather = f32[4,2,32]{2,1,0:T(2,128)S(1)} all-gather(f32[1,2,32]{2,1,0:T(2,128)} %param.37), channel_id=2, replica_groups=mesh['ctx'=4,'dp'=2,'tp'=4] {'ctx'}, dimensions={0}, use_global_device_ids=true | all-gather | bytes 1280 | tf_op jit(solution)/shard_map/all_gather | solution.py:13
  13.7 0.1 while.16
  13.8 0.1 copy.185
  13.9 2.5 %fusion.2 = bf16[2,32,64,128]{3,2,0,1:T(8,128)(2,1)} fusion(bf16[1,2,32,64,128]{4,3,2,1,0:T(8,128)(2,1)} %param.36, f32[2,32]{0,1:T(8,128)S(1)} %copy.185), kind=kLoop, calls=%fused_computation.6 | loop fusion | flops 1572864 | bytes 2097408 | tf_op jit(solution)/shard_map/convert_element_type | solution.py:67
  16.4 0.7 fusion.65
  17.1 0.8 multiply_reduce_fusion.2
  18.0 0.1 reshape.339
  18.1 0.1 copy.177
  18.2 0.1 copy.178
  18.3 6.9 %gather_fusion = bf16[16,256]{1,0:T(8,128)(2,1)S(1)} fusion(bf16[25140,256]{1,0:T(8,128)(2,1)} %param.23, s32[1024]{0:T(1024)S(1)} %pad_clamp_fusion), kind=kCustom, calls=%fused_computation | custom fusion | bytes 16448 | tf_op jit(solution)/shard_map/jit(_take)/gather | solution.py:96
  25.3 5.0 %all-reduce = bf16[4,4,256]{2,0,1:T(4,128)(2,1)S(1)} all-reduce(bf16[4,4,256]{2,0,1:T(4,128)(2,1)S(1)} %select_convert_fusion), channel_id=3, replica_groups=mesh['ctx'=4,'dp'=2,'tp'=4] {'dp'}, use_global_device_ids=true, to_apply=%region_1.2.clone | all-reduce | flops 4096 | bytes 16384
  30.3 1.2 dynamic-slice
  32.2 32.8 %all_gather.21 = bf16[4,2,4096]{2,0,1:T(4,128)(2,1)S(1)} all-gather(bf16[4,2,256]{2,0,1:T(4,128)(2,1)S(1)} %constant_dynamic-slice_fusion), channel_id=1, replica_groups=mesh['ctx'=4,'dp'=2,'tp'=4] {'ctx','tp'}, dimensions={2}, use_global_device_ids=true | all-gather | bytes 69632 | tf_op jit(solution)/shard_map/all_gather | solution.py:101
  65.0 0.1 multiply_reduce_fusion
  65.2 0.7 dynamic_slice.17
  66.0 0.7 exponential_negate_fusion
  66.6 4.6 %all_gather.26 = bf16[4,3,8,64]{3,2,1,0:T(8,128)(2,1)S(1)} all-gather(bf16[2,3,8,64]{3,2,1,0:T(8,128)(2,1)} %param.38), channel_id=1, replica_groups=mesh['ctx'=4,'dp'=2,'tp'=4] {'dp'}, dimensions={0}, use_global_device_ids=true | all-gather | bytes 18432 | tf_op jit(solution)/shard_map/all_gather | solution.py:80
  71.2 0.1 copy.181
  71.3 0.1 rsqrt.15
  71.4 0.1 reshape.335
  71.5 0.2 convolution_bitcast_fusion.2
  71.8 6.8 %convolution_bitcast_fusion.1 = f32[2,8,8,64]{3,1,2,0:T(8,128)S(1)} fusion(bf16[2,8,64,4096]{3,2,1,0:T(8,128)(2,1)} %param.25, f32[8,4096]{1,0:T(8,128)S(1)} %reshape.335, f32[4096]{0:T(1024)S(1)} %copy-done.2, f32[8]{0:T(128)S(1)} %rsqrt.15), kind=kOutput, calls=%fused_computation.9 | convolution fusion | flops 67207168 | bytes 8568864 | tf_op jit(solution)/shard_map/rd,khed->krhe/dot_general | solution.py:105
  78.6 28.9 %all-gather.1 = f32[16,24,8]{1,2,0:T(8,128)S(1)} all-gather(f32[1,24,8]{1,2,0:T(8,128)S(1)} %convolution_bitcast_fusion.2), channel_id=1, replica_groups=mesh['ctx'=4,'dp'=2,'tp'=4] {'ctx','tp'}, dimensions={0}, use_global_device_ids=true | all-gather | bytes 13056 | tf_op jit(solution)/shard_map/all_gather | solution.py:109
  107.6 0.1 reshape.348
  107.7 0.2 fusion.26
  107.9 0.1 multiply_exponential_fusion.3
  108.1 0.1 copy.183
  108.2 0.1 copy.195
  108.3 0.1 copy.198
  108.3 0.1 copy.201
  108.5 0.1 fusion.19
  108.6 0.1 broadcast_multiply_fusion.3
  108.7 0.2 copy.192
  108.8 0.2 copy.197
  109.0 0.2 copy.200
  109.2 0.2 copy.203
  109.3 4.4 %all_gather.27 = bf16[4,3,256]{2,1,0:T(4,128)(2,1)S(1)} all-gather(bf16[2,3,256]{2,1,0:T(4,128)(2,1)S(1)} %copy.193), channel_id=1, replica_groups=mesh['ctx'=4,'dp'=2,'tp'=4] {'dp'}, dimensions={0}, use_global_device_ids=true | all-gather | bytes 9216 | tf_op jit(solution)/shard_map/all_gather | solution.py:83
  113.7 0.2 fusion.55
  114.0 3.4 %all-to-all-start = ((bf16[2,32,16,128]{3,2,0,1:T(8,128)(2,1)}), bf16[2,32,16,128]{3,2,0,1:T(8,128)(2,1)S(1)}, u32[]{:S(2)}, u32[]{:S(2)}) async-start(bf16[2,32,16,128]{3,2,0,1:T(8,128)(2,1)} %reduce-scatter.8.cloned.1.call-done), calls=%async_computation.1 | async-start | bytes 524288 | tf_op jit(solution)/shard_map/all_to_all | solution.py:69
  117.5 5.9 %all-to-all-done = bf16[2,32,16,128]{3,2,0,1:T(8,128)(2,1)S(1)} async-done(((bf16[2,32,16,128]{3,2,0,1:T(8,128)(2,1)}), bf16[2,32,16,128]{3,2,0,1:T(8,128)(2,1)S(1)}, u32[]{:S(2)}, u32[]{:S(2)}) %all-to-all-start) | async-done | bytes 262176 | tf_op jit(solution)/shard_map/all_to_all | solution.py:69
  123.4 8.4 %all_gather.25 = bf16[4,8,64,128]{3,2,1,0:T(8,128)(2,1)S(1)} all-gather(bf16[2,8,64,128]{3,2,1,0:T(8,128)(2,1)S(1)} %bitcast.312), channel_id=1, replica_groups=mesh['ctx'=4,'dp'=2,'tp'=4] {'dp'}, dimensions={0}, use_global_device_ids=true | all-gather | bytes 786432 | tf_op jit(solution)/shard_map/all_gather | solution.py:77
  131.9 3.2 %multiply_add_fusion = (f32[2,8,64,128]{3,0,2,1:T(2,128)S(1)}, bf16[2,8,64,128]{3,0,2,1:T(2,128)(2,1)S(1)}, bf16[2,8,64,128]{3,0,2,1:T(2,128)(2,1)S(1)}, bf16[2,8,64,128]{3,0,2,1:T(2,128)(2,1)S(1)}) fusion(f32[2,128]{1,0:T(2,128)S(1)} %get-tuple-element.228, f32[2,8,64]{0,2,1:T(8,128)S(1)} %copy.203, f32[2,8]{0,1:T(8,128)S(1)} %copy.201, ...), kind=kOutput, calls=%fused_computation.17 | convolution fusion | flops 3014664 | bytes 1855752 | tf_op jit(solution)/shard_map/dot_general | solution.py:30
  135.1 0.3 fusion.81
  135.4 0.3 fusion.4
  135.7 0.3 fusion.6
  136.1 0.3 fusion.8
  136.4 0.1 multiply_bitcast_fusion.3
  136.5 0.1 multiply_reduce_fusion.1
  136.6 0.1 copy.204
  136.7 10.6 %psum.14 = f32[4,2]{0,1:T(2,128)S(1)} all-reduce(f32[4,2]{0,1:T(2,128)S(1)} %copy.204), channel_id=1, replica_groups=mesh['ctx'=4,'dp'=2,'tp'=4] {'tp'}, use_global_device_ids=true, to_apply=%region_7.8 | all-reduce | flops 8 | bytes 64 | tf_op jit(solution)/shard_map/psum | solution.py:145
  147.3 5.6 %psum.15 = f32[4,2]{0,1:T(2,128)S(1)} all-reduce(f32[4,2]{0,1:T(2,128)S(1)} %psum.14), channel_id=1, replica_groups=mesh['ctx'=4,'dp'=2,'tp'=4] {'ctx'}, use_global_device_ids=true, to_apply=%region_8.9 | all-reduce | flops 8 | bytes 64 | tf_op jit(solution)/shard_map/psum | solution.py:145
  153.0 0.1 copy.205
  153.1 2.9 %fusion = bf16[4,2,4096]{2,0,1:T(4,128)(2,1)S(1)} fusion(bf16[8,64,4096]{2,1,0:T(8,128)(2,1)} %param.35, bf16[4,2,8,64]{3,2,1,0:T(8,128)(2,1)S(1)} %multiply_convert_fusion.1), kind=kOutput, calls=%fused_computation.3 | convolution fusion | flops 33587200 | bytes 4268032 | tf_op jit(solution)/shard_map/tphe,hed->tpd/dot_general | solution.py:148
  156.0 2.9 %copy.279 = bf16[4,2,4096]{0,1,2:T(2,128)(2,1)S(1)} copy(bf16[4,2,4096]{2,0,1:T(4,128)(2,1)S(1)} %fusion) | data formatting | bytes 131072
  159.0 1.8 reshape.378
  160.8 22.4 %reduce-scatter.10.cloned.1.call-done = bf16[1024,8]{1,0:T(8,128)(2,1)} async-done(((bf16[4096,8]{1,0:T(8,128)(2,1)}), bf16[1024,8]{1,0:T(8,128)(2,1)}) %reduce-scatter.10.cloned.1.call-update) | async-done | bytes 16400
  183.2 1.2 reshape.379
  184.4 0.4 copy.280
  184.8 0.5 copy.281
  185.3 1.4 reshape.380
  186.7 22.0 %reduce-scatter.12.cloned.1.call-done = f32[256,8]{1,0:T(8,128)} async-done(((f32[1024,8]{1,0:T(8,128)}), f32[256,8]{1,0:T(8,128)}) %reduce-scatter.12.cloned.1.call-update) | async-done | bytes 8208
  208.7 1.0 reshape.381
  209.7 0.1 copy.282
  209.8 0.6 copy.207
  (65 shorter events, 0.9 us)
Async XLA Ops:
  7.2 64.3 %copy-start = (bf16[4096,24]{0,1:T(8,128)(2,1)S(1)}, bf16[4096,24]{0,1:T(8,128)(2,1)}, u32[]{:S(2)}) copy-start(bf16[4096,24]{0,1:T(8,128)(2,1)} %param.26) | copy-start | bytes 589828
  7.2 64.3 %copy-start.2 = (f32[4096]{0:T(1024)S(1)}, f32[4096]{0:T(1024)}, u32[]{:S(2)}) copy-start(f32[4096]{0:T(1024)} %param.24) | copy-start | bytes 49156
  7.2 106.8 %reduce-scatter.8.cloned.1.call-start = ((), (), s32[]{:S(2)}) async-start(), calls=%async_computation.4 | async-start | bytes 1310720 | tf_op jit(solution)/shard_map/reduce_scatter | solution.py:66
  71.8 36.2 %copy-start.10 = (f32[8]{0:T(128)S(1)}, f32[8]{0:T(128)}, u32[]{:S(2)}) copy-start(f32[8]{0:T(128)} %param.31) | copy-start | bytes 100
  71.8 36.3 %copy-start.7 = (bf16[2,3,256]{2,0,1:T(2,128)(2,1)S(1)}, bf16[2,3,256]{2,0,1:T(2,128)(2,1)}, u32[]{:S(2)}) copy-start(bf16[2,3,256]{2,0,1:T(2,128)(2,1)} %param.39) | copy-start | bytes 9220
  71.8 36.7 %copy-start.4 = (f32[4,8,64]{2,1,0:T(8,128)S(1)}, f32[4,8,64]{2,1,0:T(8,128)}, u32[]{:S(2)}) copy-start(f32[4,8,64]{2,1,0:T(8,128)} %param.27) | copy-start | bytes 24580
  71.8 36.8 %copy-start.3 = (f32[8,64]{1,0:T(8,128)S(1)}, f32[8,64]{1,0:T(8,128)}, u32[]{:S(2)}) copy-start(f32[8,64]{1,0:T(8,128)} %param.28) | copy-start | bytes 6148
  71.8 42.1 %copy-start.6 = (f32[4,256]{1,0:T(4,128)S(1)}, f32[4,256]{1,0:T(4,128)}, u32[]{:S(2)}) copy-start(f32[4,256]{1,0:T(4,128)} %param.29) | copy-start | bytes 12292
  71.8 42.2 %copy-start.8 = (f32[256]{0:T(256)S(1)}, f32[256]{0:T(256)}, u32[]{:S(2)}) copy-start(f32[256]{0:T(256)} %param.30) | copy-start | bytes 3076
  114.0 9.4 %all-to-all-start = ((bf16[2,32,16,128]{3,2,0,1:T(8,128)(2,1)}), bf16[2,32,16,128]{3,2,0,1:T(8,128)(2,1)S(1)}, u32[]{:S(2)}, u32[]{:S(2)}) async-start(bf16[2,32,16,128]{3,2,0,1:T(8,128)(2,1)} %reduce-scatter.8.cloned.1.call-done), calls=%async_computation.1 | async-start | bytes 524288 | tf_op jit(solution)/shard_map/all_to_all | solution.py:69
  117.5 65.8 %reduce-scatter.10.cloned.1.call-start = ((), (), s32[]{:S(2)}) async-start(), calls=%async_computation.5 | async-start | bytes 1310720
  131.9 4.5 %copy-start.9 = (f32[8]{0:T(128)S(1)}, f32[8]{0:T(128)}, u32[]{:S(2)}) copy-start(f32[8]{0:T(128)} %param.33) | copy-start | bytes 100
  131.9 21.2 %copy-start.5 = (f32[8,64]{1,0:T(8,128)S(1)}, f32[8,64]{1,0:T(8,128)}, u32[]{:S(2)}) copy-start(f32[8,64]{1,0:T(8,128)} %param.34) | copy-start | bytes 6148
  135.1 23.9 %copy-start.1 = (f32[2,8,64,128]{3,2,1,0:T(8,128)}, f32[2,8,64,128]{3,2,1,0:T(8,128)S(1)}, u32[]{:S(2)}) copy-start(f32[2,8,64,128]{3,2,1,0:T(8,128)S(1)} %copy.208) | copy-start | bytes 1572868
  160.8 47.9 %reduce-scatter.12.cloned.1.call-start = ((), (), s32[]{:S(2)}) async-start(), calls=%async_computation.6 | async-start | bytes 655360
Sparse Core Ops, SparseCore 0:
  16.5 26.5 reduce-scatter.7
  160.9 22.2 reduce-scatter.9
  186.8 21.8 reduce-scatter.11
